TPU v7x, 32 devices: a whole 2x2x4 slice. The times are simulated.
32 devices in a mesh: section: 2 (over x), dp: 4 (over z), fsdp: 4 (over y, core).
Axes of the slice: x: 2, y: 2, z: 4, core: 2. Of those that a mesh axis runs over, the one named last changes fastest.
Arguments:
- inputs: float32 [32, 128, 1536], P(('dp', 'fsdp')), may hold values from -6 to 6
- cotangent: float32 [32, 128, 1536], P(('dp', 'fsdp')), may hold values from -6 to 6
- lengths: int32 [32], P(('dp', 'fsdp')), may hold values from 1 to 128, 2560 in all
- norm_gain: float32 [2, 1536], P('section'), may hold values from 0.5 to 1.5
- in_weight: bfloat16 [2, 1536, 6400], P('section', 'fsdp'), may hold values from -0.15625 to 0.15625
- dt_weight: bfloat16 [2, 1536, 48], P('section', 'fsdp'), may hold values from -0.15625 to 0.15625
- conv_weight: float32 [2, 4, 3328], P('section'), may hold values from -3 to 3
- conv_bias: float32 [2, 3328], P('section'), may hold values from -0.5 to 0.5
- dt_bias: float32 [2, 48], P('section'), may hold values from -4 to -1
- decay_log: float32 [2, 48], P('section'), may hold values from -4.6 to 0
- skip_gain: float32 [2, 48], P('section'), may hold values from 0.5 to 1.5
- gate_gain: float32 [2, 3072], P('section'), may hold values from 0.5 to 1.5
- out_weight: bfloat16 [2, 3072, 1536], P('section', 'fsdp'), may hold values from -0.109375 to 0.109375
Outputs:
- layer_outputs: float32 [2, 32, 128, 1536], P('section', ('dp', 'fsdp'))
- input_grads: float32 [2, 32, 128, 1536], P('section', ('dp', 'fsdp'))
- grad_norm_gain: float32 [2, 1536], P('section')
- grad_in_weight: float32 [2, 1536, 6400], P('section', 'fsdp')
- grad_dt_weight: float32 [2, 1536, 48], P('section', 'fsdp')
- grad_conv_weight: float32 [2, 4, 3328], P('section')
- grad_conv_bias: float32 [2, 3328], P('section')
- grad_dt_bias: float32 [2, 48], P('section')
- grad_decay_log: float32 [2, 48], P('section')
- grad_skip_gain: float32 [2, 48], P('section')
- grad_gate_gain: float32 [2, 3072], P('section')
- grad_out_weight: float32 [2, 3072, 1536], P('section', 'fsdp')
Inputs may be any that keep to these rules, and one draw needn't show every extreme that they name: `lengths`: positions from a sequence's length on are padding.
All inputs are finite; a program needn't handle non-finite values. No bound on the sum of `lengths` on one device may be relied on, other than what follows from the above.
Results may differ from a plain program's by a relative error of at most 0.011.
Values may be sent and summed in bfloat16 or wider, within the bound.
No kernel may reach another device: no remote copies, remote signals or barrier semaphores. Data moves between devices by JAX's collectives and lax.ppermute only.
A program may use at most 448 MiB of HBM per device.

v0:
```python
import jax
import jax.numpy as jnp
from jax import lax
from jax.sharding import PartitionSpec as P

INNER = 3072
HEADS = 48
HEAD_DIM = 64
STATE = 128
BLOCK = 64
CONV = 4
BUCKET = 128
MICRO = 2
epsilon = 1e-05
highest = lax.Precision.HIGHEST


def passed_along(block, axis, distance):
    devices = range(lax.axis_size(axis))
    route = [(i - distance, i) for i in devices if i - distance in devices]
    return lax.ppermute(block, axis, route)


def front_norm(residual, norm_gain):
    inverse = lax.rsqrt(jnp.mean(residual * residual, axis=-1, keepdims=True) + epsilon)
    return residual * inverse * norm_gain


def state_space(values, step_sizes, log_decay, inputs_b, outputs_c, skip_gain):
    seq_count, length = (values.shape[0], values.shape[1])
    blocks = length // BLOCK
    values_k = values.reshape(seq_count, blocks, BLOCK, HEADS, HEAD_DIM)
    steps_k = step_sizes.reshape(seq_count, blocks, BLOCK, HEADS)
    totals = jnp.cumsum(log_decay.reshape(seq_count, blocks, BLOCK, HEADS), axis=2)
    in_k = inputs_b.reshape(seq_count, blocks, BLOCK, STATE)
    out_k = outputs_c.reshape(seq_count, blocks, BLOCK, STATE)
    causal = (
        jnp.arange(BLOCK, dtype=jnp.int32)[:, None] >= jnp.arange(BLOCK, dtype=jnp.int32)[None, :]
    )[None, None, :, :, None]
    spread = totals[:, :, :, None, :] - totals[:, :, None, :, :]
    kernel = jnp.where(causal, jnp.exp(jnp.where(causal, spread, 0.0)), 0.0)
    inner_cb = jnp.einsum("skin,skjn->skij", out_k, in_k, precision=highest)
    weighted = inner_cb[..., None] * kernel * steps_k[:, :, None, :, :]
    local_part = jnp.einsum("skijh,skjhp->skihp", weighted, values_k, precision=highest)
    to_end = jnp.exp(totals[:, :, -1:, :] - totals) * steps_k
    scaled_values = values_k * to_end[..., None]
    block_states = jnp.einsum("skjhp,skjn->skhpn", scaled_values, in_k, precision=highest)
    carried = jnp.zeros((seq_count, HEADS, HEAD_DIM, STATE), jnp.float32)
    entering = []
    for block_index in range(blocks):
        entering.append(carried)
        carried = (
            jnp.exp(totals[:, block_index, -1, :])[:, :, None, None] * carried
            + block_states[:, block_index]
        )
    entering_all = jnp.stack(entering, axis=1)
    carried_part = (
        jnp.einsum("skin,skhpn->skihp", out_k, entering_all, precision=highest)
        * jnp.exp(totals)[..., None]
    )
    result = (local_part + carried_part).reshape(seq_count, length, HEADS, HEAD_DIM)
    return result + skip_gain[:, None] * values


def mixer_core(projected, dt_raw, conv_weight, conv_bias, dt_bias, decay_log, skip_gain, gate_gain):
    row_count = projected.shape[0]
    seq_count = row_count // BUCKET
    shaped = projected.reshape(seq_count, BUCKET, projected.shape[1])
    gate_part = shaped[:, :, :INNER]
    conv_input = shaped[:, :, INNER:]
    padded = jnp.pad(conv_input, ((0, 0), (CONV - 1, 0), (0, 0)))
    convolved = conv_bias + conv_weight[0] * padded[:, 0:BUCKET]
    for offset in range(1, CONV):
        convolved = convolved + conv_weight[offset] * padded[:, offset : offset + BUCKET]
    activated = jax.nn.silu(convolved)
    values = activated[:, :, :INNER].reshape(seq_count, BUCKET, HEADS, HEAD_DIM)
    inputs_b = activated[:, :, INNER : INNER + STATE]
    outputs_c = activated[:, :, INNER + STATE :]
    step_sizes = jax.nn.softplus(dt_raw.reshape(seq_count, BUCKET, HEADS) + dt_bias)
    log_decay = -jnp.exp(decay_log) * step_sizes
    scanned = state_space(values, step_sizes, log_decay, inputs_b, outputs_c, skip_gain).reshape(
        seq_count, BUCKET, INNER
    )
    gated_out = scanned * jax.nn.silu(gate_part)
    inverse = lax.rsqrt(jnp.mean(gated_out * gated_out, axis=-1, keepdims=True) + epsilon)
    return (gated_out * inverse * gate_gain).reshape(row_count, INNER)


def layer_forward(residual, params):
    norm_gain, in_weight, dt_weight, small_params, out_weight = params
    normed = front_norm(residual, norm_gain).astype(jnp.bfloat16)
    projected = jnp.dot(normed, in_weight, preferred_element_type=jnp.float32)
    dt_raw = jnp.dot(normed, dt_weight, preferred_element_type=jnp.float32)
    mixed_out = mixer_core(projected, dt_raw, *small_params).astype(jnp.bfloat16)
    output = residual + jnp.dot(mixed_out, out_weight, preferred_element_type=jnp.float32)
    return (output, (normed, projected, dt_raw, mixed_out))


def contract_rows(left, right):
    return lax.dot_general(
        left, right, (((0,), (0,)), ((), ())), preferred_element_type=jnp.float32
    )


def contract_cols(left, right):
    return lax.dot_general(
        left, right, (((1,), (1,)), ((), ())), preferred_element_type=jnp.float32
    )


def column_term(columns, grads):
    return contract_rows(columns, grads)


def reorder(columns, data_groups, owners):
    row_count, total_cols = columns.shape
    shaped = columns.reshape(row_count, owners, data_groups, total_cols // (owners * data_groups))
    return shaped.transpose(0, 2, 1, 3).reshape(row_count, total_cols)


def per_device(
    inputs,
    cotangent,
    lengths,
    norm_gain,
    in_weight,
    dt_weight,
    conv_weight,
    conv_bias,
    dt_bias,
    decay_log,
    skip_gain,
    gate_gain,
    out_weight,
):
    first_section = lax.axis_index("section") == 0
    full_in, full_dt, full_out = (
        lax.all_gather(in_weight[0], "fsdp", axis=0, tiled=True),
        lax.all_gather(dt_weight[0], "fsdp", axis=0, tiled=True),
        lax.all_gather(out_weight[0], "fsdp", axis=0, tiled=True),
    )
    small_params = (
        conv_weight[0],
        conv_bias[0],
        dt_bias[0],
        decay_log[0],
        skip_gain[0],
        gate_gain[0],
    )
    own_gain = norm_gain[0]
    params = (own_gain, full_in, full_dt, small_params, full_out)
    per_micro = inputs.shape[0] // MICRO
    row_count = per_micro * BUCKET
    model_width = inputs.shape[2]
    proj_cols = full_in.shape[1]
    data_groups = lax.axis_size("dp")
    owners = lax.axis_size("fsdp")
    positions = jnp.arange(BUCKET, dtype=jnp.int32)
    empty_rows = jnp.zeros((row_count, model_width), jnp.float32)

    def micro_rows(source, micro_index):
        return source[micro_index * per_micro : (micro_index + 1) * per_micro].reshape(
            row_count, model_width
        )

    def arrange(columns):
        return reorder(columns, data_groups, owners)

    layer_inputs = []
    results = []
    kept_all = []
    for section_tick in range(MICRO + 1):
        if section_tick > 0:
            arrived = passed_along(results[-1], "section", 1)
        else:
            arrived = empty_rows
        own_rows = micro_rows(inputs, section_tick) if section_tick < MICRO else empty_rows
        residual = jnp.where(first_section, own_rows, arrived)
        output, kept_values = layer_forward(residual, params)
        layer_inputs.append(residual)
        results.append(output)
        kept_all.append(kept_values)
    small_acc = (jnp.zeros(own_gain.shape, jnp.float32),) + tuple(
        (jnp.zeros(a.shape, jnp.float32) for a in small_params)
    )
    total_in = None
    total_out = None
    grads_back = []
    for section_tick in range(MICRO + 1):
        if section_tick > 0:
            returned = passed_along(grads_back[-1], "section", -1)
        else:
            returned = empty_rows
        if section_tick < MICRO:
            own_lengths = lengths[section_tick * per_micro : (section_tick + 1) * per_micro]
            live_rows = (positions[None, :] < own_lengths[:, None]).astype(jnp.float32)
            top_grad = micro_rows(cotangent, section_tick) * live_rows.reshape(row_count, 1)
        else:
            top_grad = empty_rows
        later_tick = min(section_tick + 1, MICRO)
        earlier = max(section_tick - 1, 0)
        grad_output = jnp.where(first_section, returned, top_grad)
        residual = jnp.where(first_section, layer_inputs[earlier], layer_inputs[later_tick])
        normed, projected, dt_raw, mixed_out = jax.tree.map(
            lambda a, b: jnp.where(first_section, a, b), kept_all[earlier], kept_all[later_tick]
        )
        grad_rounded = grad_output.astype(jnp.bfloat16)
        grad_mixed = contract_cols(grad_rounded, full_out)
        _, pull_mixer = jax.vjp(mixer_core, projected, dt_raw, *small_params)
        pulled = pull_mixer(grad_mixed)
        grad_proj = pulled[0].astype(jnp.bfloat16)
        grad_dt = pulled[1].astype(jnp.bfloat16)
        grad_cat = jnp.concatenate([grad_proj, grad_dt], axis=1)
        grad_normed = contract_cols(grad_proj, full_in) + contract_cols(grad_dt, full_dt)
        _, pull_front = jax.vjp(front_norm, residual, own_gain)
        grad_residual, grad_gain = pull_front(grad_normed)
        grads_back.append(grad_output + grad_residual)
        small_acc = tuple((a + b for a, b in zip(small_acc, (grad_gain,) + tuple(pulled[2:]))))
        normed_cols = arrange(normed)
        mixed_cols = arrange(mixed_out)
        part_in = lax.psum_scatter(
            column_term(normed_cols, grad_cat), ("dp", "fsdp"), scatter_dimension=0, tiled=True
        )
        part_out = lax.psum_scatter(
            column_term(mixed_cols, grad_rounded), ("dp", "fsdp"), scatter_dimension=0, tiled=True
        )
        total_in = part_in if total_in is None else total_in + part_in
        total_out = part_out if total_out is None else total_out + part_out
    owned_in, owned_out = (
        lax.all_gather(total_in, "dp", axis=0, tiled=True),
        lax.all_gather(total_out, "dp", axis=0, tiled=True),
    )
    small_total = lax.psum(small_acc, ("dp", "fsdp"))
    layer_out = jnp.concatenate(
        [
            jnp.where(first_section, results[m], results[m + 1]).reshape(
                per_micro, BUCKET, model_width
            )
            for m in range(MICRO)
        ],
        axis=0,
    )
    input_grad = jnp.concatenate(
        [
            jnp.where(first_section, grads_back[m + 1], grads_back[m]).reshape(
                per_micro, BUCKET, model_width
            )
            for m in range(MICRO)
        ],
        axis=0,
    )
    grad_in_part = owned_in[:, :proj_cols]
    grad_dt_part = owned_in[:, proj_cols:]
    return (
        layer_out[None],
        input_grad[None],
        small_total[0][None],
        grad_in_part[None],
        grad_dt_part[None],
        small_total[1][None],
        small_total[2][None],
        small_total[3][None],
        small_total[4][None],
        small_total[5][None],
        small_total[6][None],
        owned_out[None],
    )


def solution(mesh):
    in_specs = (
        P(("dp", "fsdp"), None, None),
        P(("dp", "fsdp"), None, None),
        P(("dp", "fsdp")),
        P("section", None),
        P("section", "fsdp", None),
        P("section", "fsdp", None),
        P("section", None, None),
        P("section", None),
        P("section", None),
        P("section", None),
        P("section", None),
        P("section", None),
        P("section", "fsdp", None),
    )
    out_specs = (
        P("section", ("dp", "fsdp"), None, None),
        P("section", ("dp", "fsdp"), None, None),
        P("section", None),
        P("section", "fsdp", None),
        P("section", "fsdp", None),
        P("section", None, None),
        P("section", None),
        P("section", None),
        P("section", None),
        P("section", None),
        P("section", None),
        P("section", "fsdp", None),
    )
    return jax.shard_map(
        per_device, mesh=mesh, in_specs=in_specs, out_specs=out_specs, check_vma=False
    )
```

profile of v0, /device:TPU:0, one launch (start us, length us, event | category | flops | bytes accessed | tf_op | source)
XLA Modules:
  0.0 1780.0 jit_solution(17367377292099813090)
XLA Ops:
  19.5 117.1 %all-gather.12.cloned.1.call-done = bf16[1,1536,6400]{2,1,0:T(8,128)(2,1)} async-done(((bf16[1,384,6400]{2,1,0:T(8,128)(2,1)}), bf16[1,1536,6400]{2,1,0:T(8,128)(2,1)}) %all-gather.12.cloned.1.call-update) | async-done | bytes 19660816 | tf_op jit(solution)/shard_map/all_gather | solution.py:138
  136.7 8.1 fusion.10
  184.4 18.1 %all-gather.14.cloned.1.call-done = bf16[1,3072,1536]{2,1,0:T(8,128)(2,1)} async-done(((bf16[1,768,1536]{2,1,0:T(8,128)(2,1)}), bf16[1,3072,1536]{2,1,0:T(8,128)(2,1)}) %all-gather.14.cloned.1.call-update) | async-done | bytes 9437200 | tf_op jit(solution)/shard_map/all_gather | solution.py:140
  214.1 14.1 collective-permute-done
  231.9 8.2 fusion.8
  310.2 8.7 fusion.396
  321.8 8.4 fusion.6
  388.8 9.2 fusion.241
  464.4 10.0 fusion.225
  571.6 14.4 fusion.4
  643.2 11.1 fusion.227
  681.2 8.2 fusion.344
  754.3 14.3 fusion.2
  792.6 21.3 %add_add_fusion.1 = f32[3072,1536]{1,0:T(8,128)} fusion(f32[3072,1536]{1,0:T(8,128)} %fusion.396, f32[3072,1536]{1,0:T(8,128)} %fusion.404, bf16[128,3072]{0,1:T(8,128)(2,1)} %bitcast.975, f32[128,1536]{1,0:T(8,128)} %collective-permute-done.3, pred[]{:T(512)S(6)} %eq.9), kind=kOutput, calls=%fused_computation.13 | convolution fusion | flops 1217593344 | bytes 58195968 | tf_op jit(solution)/shard_map/dot_general | solution.py:100
  834.1 19.9 %fusion.213 = f32[1536,6448]{1,0:T(8,128)} fusion(bf16[128,1536]{0,1:T(8,128)(2,1)S(1)} %bitcast.1029, bf16[128,48]{1,0:T(8,128)(2,1)} %bitcast.1059, bf16[128,6400]{1,0:T(8,128)(2,1)} %copy-done.45), kind=kOutput, calls=%fused_computation.278 | convolution fusion | flops 2538758144 | bytes 41660416 | tf_op jit(solution)/shard_map/dot_general | solution.py:100
  854.0 17.7 fusion.217
  921.3 10.7 fusion.229
  967.9 40.4 %add_add_fusion = f32[1536,6448]{1,0:T(8,128)} fusion(f32[1536,6448]{1,0:T(8,128)} %fusion.213, f32[1536,6448]{1,0:T(8,128)} %fusion.217, bf16[128,1536]{0,1:T(8,128)(2,1)S(1)} %bitcast.994, bf16[128,48]{1,0:T(8,128)(2,1)S(1)} %bitcast.1058, bf16[128,6400]{1,0:T(8,128)(2,1)S(1)} %fusion.232), kind=kOutput, calls=%fused_computation | convolution fusion | flops 2558566400 | bytes 120893440 | tf_op jit(solution)/shard_map/dot_general | solution.py:100
  1009.5 390.6 %reduce-scatter.3.cloned.1.call-done = f32[96,6448]{1,0:T(8,128)} async-done(((f32[1536,6448]{1,0:T(8,128)}), f32[96,6448]{1,0:T(8,128)}) %reduce-scatter.3.cloned.1.call-update) | async-done | bytes 2476048 | tf_op jit(solution)/shard_map/reduce_scatter | solution.py:221
  1414.6 10.4 fusion
  1433.2 56.9 %all-gather.10.cloned.1.call-done = f32[768,1536]{1,0:T(8,128)} async-done(((f32[192,1536]{1,0:T(8,128)}), f32[768,1536]{1,0:T(8,128)}) %all-gather.10.cloned.1.call-update) | async-done | bytes 4718608 | tf_op jit(solution)/shard_map/all_gather | solution.py:231
  1490.0 176.3 %all-gather.8.cloned.1.call-done = f32[384,6448]{1,0:T(8,128)} async-done(((f32[96,6448]{1,0:T(8,128)}), f32[384,6448]{1,0:T(8,128)}) %all-gather.8.cloned.1.call-update) | async-done | bytes 9904144 | tf_op jit(solution)/shard_map/all_gather | solution.py:230
  1666.3 8.3 slice_bitcast_fusion
  1676.3 83.1 %all-reduce.63.cloned.1.call-done = (f32[1,1536]{1,0:T(1,128)}, f32[1,4,3328]{2,1,0:T(4,128)}, f32[1,3328]{1,0:T(1,128)}, f32[1,48]{1,0:T(1,128)}, f32[1,48]{1,0...) async-done(((f32[1,1536]{1,0:T(1,128)}, f32[1,4,3328]{2,1,0:T(4,128)}, f32[1,3328]{1,0:T(1,128)}, f32[1,48]{1,0:T(1,128)}, f32[1,48]{1,0:T(1,128)}, ...) | async-done | bytes 85584 | tf_op jit(solution)/shard_map/psum | solution.py:233
  (949 shorter events, 676.6 us)
Async XLA Ops:
  7.2 129.5 %all-gather.12.cloned.1.call-start = ((), (), s32[]{:S(2)}) async-start(), calls=%async_computation.4 | async-start | bytes 24576000 | tf_op jit(solution)/shard_map/all_gather | solution.py:138
  8.0 194.5 %all-gather.14.cloned.1.call-start = ((), (), s32[]{:S(2)}) async-start(), calls=%async_computation.5 | async-start | bytes 11796480 | tf_op jit(solution)/shard_map/all_gather | solution.py:140
  8.7 1000.7 %reduce-scatter.5.cloned.1.call-start = ((), (), s32[]{:S(2)}) async-start(), calls=%async_computation.7 | async-start | bytes 20054016 | tf_op jit(solution)/shard_map/reduce_scatter | solution.py:224
  8.8 221.1 %copy-start.142 = (f32[1536]{0:T(1024)}, f32[1536]{0:T(1024)S(1)}, u32[]{:S(2)}) copy-start(f32[1536]{0:T(1024)S(1)} %reduce.80) | copy-start | bytes 18436
  8.9 137.6 %copy-start.211 = (f32[3328]{0:T(1024)}, f32[3328]{0:T(1024)S(1)}, u32[]{:S(2)}) copy-start(f32[3328]{0:T(1024)S(1)} %reduce.78) | copy-start | bytes 39940
  15.5 753.1 %copy-start.78 = (bf16[1,1536,48]{1,2,0:T(8,128)(2,1)}, bf16[1,1536,48]{1,2,0:T(8,128)(2,1)S(1)}, u32[]{:S(2)}) copy-start(bf16[1,1536,48]{1,2,0:T(8,128)(2,1)S(1)} %all-gather.1) | copy-start | bytes 442372
  15.7 129.1 %copy-start.261 = (f32[128]{0:T(128)}, f32[128]{0:T(128)S(1)}, u32[]{:S(2)}) copy-start(f32[128]{0:T(128)S(1)} %add_rsqrt_fusion.5) | copy-start | bytes 1540
  15.7 230.8 %copy-start.253 = (f32[48]{0:T(128)}, f32[48]{0:T(128)S(1)}, u32[]{:S(2)}) copy-start(f32[48]{0:T(128)S(1)} %bitcast_negate_fusion) | copy-start | bytes 580
  16.2 230.4 %copy-start.140 = (f32[128,48]{1,0:T(8,128)}, f32[128,48]{1,0:T(8,128)S(1)}, u32[]{:S(2)}) copy-start(f32[128,48]{1,0:T(8,128)S(1)} %get-tuple-element.253) | copy-start | bytes 73732
  19.3 268.4 %copy-start.135 = (f32[3072]{0:T(1024)}, f32[3072]{0:T(1024)S(1)}, u32[]{:S(2)}) copy-start(f32[3072]{0:T(1024)S(1)} %mul.1954) | copy-start | bytes 36868
  19.3 249.1 %copy-start.194 = (pred[64,64]{1,0:T(8,128)(4,1)}, pred[64,64]{1,0:T(8,128)(4,1)S(1)}, u32[]{:S(2)}) copy-start(pred[64,64]{1,0:T(8,128)(4,1)S(1)} %iota_compare_fusion) | copy-start | bytes 12292
  19.5 220.8 %copy-start.147 = (f32[3328]{0:T(1024)}, f32[3328]{0:T(1024)S(1)}, u32[]{:S(2)}) copy-start(f32[3328]{0:T(1024)S(1)} %get-tuple-element.111) | copy-start | bytes 39940
  19.5 220.8 %copy-start.152 = (f32[3328]{0:T(1024)}, f32[3328]{0:T(1024)S(1)}, u32[]{:S(2)}) copy-start(f32[3328]{0:T(1024)S(1)} %get-tuple-element.112) | copy-start | bytes 39940
  19.5 220.8 %copy-start.157 = (f32[3328]{0:T(1024)}, f32[3328]{0:T(1024)S(1)}, u32[]{:S(2)}) copy-start(f32[3328]{0:T(1024)S(1)} %get-tuple-element.113) | copy-start | bytes 39940
  19.5 220.8 %copy-start.162 = (f32[3328]{0:T(1024)}, f32[3328]{0:T(1024)S(1)}, u32[]{:S(2)}) copy-start(f32[3328]{0:T(1024)S(1)} %get-tuple-element.114) | copy-start | bytes 39940
  207.6 20.6 %collective-permute-start = (f32[128,1536]{1,0:T(8,128)S(1)}, f32[128,1536]{1,0:T(8,128)S(1)}, u32[]{:S(2)}, u32[]{:S(2)}) collective-permute-start(f32[128,1536]{1,0:T(8,128)S(1)} %fusion.150), channel_id=1, source_target_pairs={{0,16},{1,17},{2,18},{3,19},{4,20},{5,21},{6,22},{7,23},{8,24},{9,... | collective-permute-start | bytes 2359304 | tf_op jit(solution)/shard_map/ppermute | solution.py:21
  297.5 21.3 %collective-permute-start.1 = (f32[128,1536]{1,0:T(8,128)S(1)}, f32[128,1536]{1,0:T(8,128)S(1)}, u32[]{:S(2)}, u32[]{:S(2)}) collective-permute-start(f32[128,1536]{1,0:T(8,128)S(1)} %fusion.153), channel_id=1, source_target_pairs={{0,16},{1,17},{2,18},{3,19},{4,20},{5,21},{6,22},{7,23},{8,24},{9,... | collective-permute-start | bytes 2359304 | tf_op jit(solution)/shard_map/ppermute | solution.py:21
  589.5 20.9 %collective-permute-start.2 = (f32[128,1536]{1,0:T(8,128)}, f32[128,1536]{1,0:T(8,128)}, u32[]{:S(2)}, u32[]{:S(2)}) collective-permute-start(f32[128,1536]{1,0:T(8,128)} %fusion.374), channel_id=1, source_target_pairs={{16,0},{17,1},{18,2},{19,3},{20,4},{21,5},{22,6},{23,7},{24,8},{25... | collective-permute-start | bytes 2359304 | tf_op jit(solution)/shard_map/ppermute | solution.py:21
  772.7 19.9 %collective-permute-start.3 = (f32[128,1536]{1,0:T(8,128)}, f32[128,1536]{1,0:T(8,128)}, u32[]{:S(2)}, u32[]{:S(2)}) collective-permute-start(f32[128,1536]{1,0:T(8,128)} %get-tuple-element.146), channel_id=1, source_target_pairs={{16,0},{17,1},{18,2},{19,3},{20,4},{21,5},{22,6},{23,7},{24,8},{25... | collective-permute-start | bytes 2359304 | tf_op jit(solution)/shard_map/ppermute | solution.py:21
  813.9 586.2 %reduce-scatter.3.cloned.1.call-start = ((), (), s32[]{:S(2)}) async-start(), calls=%async_computation.6 | async-start | bytes 42614784 | tf_op jit(solution)/shard_map/reduce_scatter | solution.py:221
  1008.4 481.6 %all-gather.10.cloned.1.call-start = ((), (), s32[]{:S(2)}) async-start(), calls=%async_computation.3 | async-start | bytes 5898240 | tf_op jit(solution)/shard_map/all_gather | solution.py:231
  1009.4 390.9 %copy-start.81 = (f32[128,1536]{1,0:T(8,128)S(1)}, f32[128,1536]{1,0:T(8,128)}, u32[]{:S(2)}) copy-start(f32[128,1536]{1,0:T(8,128)} %copy-done.80) | copy-start | bytes 2359300
  1009.5 656.8 %all-gather.8.cloned.1.call-start = ((), (), s32[]{:S(2)}) async-start(), calls=%async_computation.2 | async-start | bytes 12533760 | tf_op jit(solution)/shard_map/all_gather | solution.py:230
  1400.2 359.1 %all-reduce.63.cloned.1.call-start = ((), (), s32[]{:S(2)}) async-start(), calls=%async_computation.8 | async-start | bytes 173056 | tf_op jit(solution)/shard_map/psum | solution.py:233
  (284 other events, 1908.2 us)
Sparse Core Ops, SparseCore 0:
  9.6 127.0 all-gather.11
  138.2 64.2 all-gather.13
  814.1 195.3 reduce-scatter.4
  1013.6 386.4 reduce-scatter.2
  1401.6 88.4 all-gather.9
  1491.4 174.7 all-gather.7
  1671.8 87.5 all-reduce.62
where the time goes:
time: 1790 us; the launch traced here: 1780 us
  waiting for transfers between devices  865 us (48%)
  matrix products  454 us (25%)
  local copies, waits for them, and re-layouts  295 us (16%)
  other arithmetic  132 us (7%)
    reduce_scatter x1, waiting for transfers between devices, per_device(): lax.psum_scatter(column_term(normed_cols, grad_cat), ('dp', 'fsdp'), scat...  391 us
    all_gather x1, waiting for transfers between devices, per_device(): lax.all_gather(total_in, 'dp', axis=0, tiled=True)  176 us
    all_gather x1, waiting for transfers between devices, per_device(): lax.all_gather(in_weight[0], 'fsdp', axis=0, tiled=True)  117 us
    dot_general x6, matrix products, contract_rows(): lax.dot_general(left, right, (((0,), (0,)), ((), ())), preferred_element_...  116 us
    dot_general x12, matrix products, state_space(): jnp.einsum('skijh,skjhp->skihp', weighted, values_k, precision=highest)  93.3 us
    psum x1, waiting for transfers between devices, per_device(): small_total = lax.psum(small_acc, ('dp', 'fsdp'))  83.1 us
    dot_general x9, matrix products, contract_cols(): lax.dot_general(left, right, (((1,), (1,)), ((), ())), preferred_element_...  67 us
    dot_general x12, matrix products, state_space(): jnp.einsum('skjhp,skjn->skhpn', scaled_values, in_k, precision=highest)  65.5 us
  transfers between devices with their start and end apart: 11, of which 10 were waited for; matrix products, arithmetic and copies ran while one was open for 18% of the time, Pallas kernels for 0%

commit v1 on v0

--- a/solution.py
+++ b/solution.py
@@ -13,6 +13,17 @@
 MICRO = 2
 epsilon = 1e-05
 highest = lax.Precision.HIGHEST
+
+
+def ring_gather(array, axis, dim):
+    ways = lax.axis_size(axis)
+    pieces = [array]
+    for far in range(1, ways):
+        pieces.append(
+            lax.ppermute(pieces[far - 1], axis, [(d, (d - 1) % ways) for d in range(ways)])
+        )
+    line = jnp.concatenate(pieces, axis=dim)
+    return jnp.roll(line, lax.axis_index(axis) * array.shape[dim], axis=dim)
 
 
 def passed_along(block, axis, distance):
@@ -227,7 +238,7 @@
         total_in = part_in if total_in is None else total_in + part_in
         total_out = part_out if total_out is None else total_out + part_out
     owned_in, owned_out = (
-        lax.all_gather(total_in, "dp", axis=0, tiled=True),
+        ring_gather(total_in, "dp", 0),
         lax.all_gather(total_out, "dp", axis=0, tiled=True),
     )
     small_total = lax.psum(small_acc, ("dp", "fsdp"))

time: 1790 us -> 1720 us (0.961)
  waiting for transfers between devices: 865 us -> 777 us
  local copies, waits for them, and re-layouts: 295 us -> 315 us
    ppermute x0 -> x3, waiting for transfers between devices: none -> 204 us  [ring_gather(): lax.ppermute(pieces[far - 1], axis, [(d, (d - 1) % ways) for d in range(w...]
    all_gather x1 -> x0, waiting for transfers between devices: 176 us -> none  [per_device(): lax.all_gather(total_in, 'dp', axis=0, tiled=True)]
    all_gather x1, waiting for transfers between devices: 56.9 us -> 0.01 us  [per_device(): lax.all_gather(total_out, 'dp', axis=0, tiled=True)]
    psum x1, waiting for transfers between devices: 83.1 us -> 29.1 us  [per_device(): small_total = lax.psum(small_acc, ('dp', 'fsdp'))]
    unnamed x603 -> x610, local copies, waits for them, and re-layouts: 48.6 us -> 66.8 us
  transfers between devices with their start and end apart: 11 -> 13, of which waited for: 10 -> 11; matrix products, arithmetic and copies ran while one was open for 18% -> 20% of each run, Pallas kernels for 0% -> 0%
where the time goes in v1:
time: 1720 us
  waiting for transfers between devices  777 us (45%)
  matrix products  453 us (26%)
  local copies, waits for them, and re-layouts  315 us (18%)
  other arithmetic  132 us (8%)
  between operations  17.8 us (1%)
    reduce_scatter x1, waiting for transfers between devices, per_device(): lax.psum_scatter(column_term(normed_cols, grad_cat), ('dp', 'fsdp'), scat...  386 us
    ppermute x3, waiting for transfers between devices, ring_gather(): lax.ppermute(pieces[far - 1], axis, [(d, (d - 1) % ways) for d in range(w...  204 us
    all_gather x1, waiting for transfers between devices, per_device(): lax.all_gather(in_weight[0], 'fsdp', axis=0, tiled=True)  117 us
    dot_general x6, matrix products, contract_rows(): lax.dot_general(left, right, (((0,), (0,)), ((), ())), preferred_element_...  116 us
    dot_general x12, matrix products, state_space(): jnp.einsum('skijh,skjhp->skihp', weighted, values_k, precision=highest)  93.2 us
    dot_general x9, matrix products, contract_cols(): lax.dot_general(left, right, (((1,), (1,)), ((), ())), preferred_element_...  67 us
    unnamed x610, local copies, waits for them, and re-layouts  66.8 us
    dot_general x12, matrix products, state_space(): jnp.einsum('skjhp,skjn->skhpn', scaled_values, in_k, precision=highest)  65.5 us
  transfers between devices with their start and end apart: 13, of which 11 were waited for; matrix products, arithmetic and copies ran while one was open for 20% of the time, Pallas kernels for 0%

profile of v1, /device:TPU:0, one launch (start us, length us, event | category | flops | bytes accessed | tf_op | source)
XLA Modules:
  0.0 1715.4 jit_solution(3765984533001470021)
XLA Ops:
  19.5 117.1 %all-gather.9.cloned.1.call-done = bf16[1,1536,6400]{2,1,0:T(8,128)(2,1)} async-done(((bf16[1,384,6400]{2,1,0:T(8,128)(2,1)}), bf16[1,1536,6400]{2,1,0:T(8,128)(2,1)}) %all-gather.9.cloned.1.call-update) | async-done | bytes 19660816 | tf_op jit(solution)/shard_map/all_gather | solution.py:149
  184.2 18.2 %all-gather.11.cloned.1.call-done = bf16[1,3072,1536]{2,1,0:T(8,128)(2,1)} async-done(((bf16[1,768,1536]{2,1,0:T(8,128)(2,1)}), bf16[1,3072,1536]{2,1,0:T(8,128)(2,1)}) %all-gather.11.cloned.1.call-update) | async-done | bytes 9437200 | tf_op jit(solution)/shard_map/all_gather | solution.py:151
  214.1 14.1 collective-permute-done
  231.9 8.2 fusion.8
  310.4 8.7 fusion.396
  322.0 8.4 fusion.6
  388.8 9.2 fusion.241
  464.4 10.0 fusion.225
  571.6 14.4 fusion.4
  643.3 11.2 fusion.227
  681.3 8.2 fusion.344
  754.4 14.3 fusion.2
  792.7 21.3 %add_add_fusion.1 = f32[3072,1536]{1,0:T(8,128)} fusion(f32[3072,1536]{1,0:T(8,128)} %fusion.396, f32[3072,1536]{1,0:T(8,128)} %fusion.404, bf16[128,3072]{0,1:T(8,128)(2,1)} %bitcast.975, f32[128,1536]{1,0:T(8,128)} %collective-permute-done.3, pred[]{:T(512)S(6)} %eq.12), kind=kOutput, calls=%fused_computation.13 | convolution fusion | flops 1217593344 | bytes 58195968 | tf_op jit(solution)/shard_map/dot_general | solution.py:111
  834.2 19.9 %fusion.213 = f32[1536,6448]{1,0:T(8,128)} fusion(bf16[128,1536]{0,1:T(8,128)(2,1)S(1)} %bitcast.1029, bf16[128,48]{1,0:T(8,128)(2,1)} %bitcast.1059, bf16[128,6400]{1,0:T(8,128)(2,1)} %copy-done.45), kind=kOutput, calls=%fused_computation.278 | convolution fusion | flops 2538758144 | bytes 41660416 | tf_op jit(solution)/shard_map/dot_general | solution.py:111
  854.2 17.7 %fusion.217 = f32[1536,6448]{1,0:T(8,128)} fusion(bf16[128,1536]{0,1:T(8,128)(2,1)} %bitcast.1030, bf16[128,48]{1,0:T(8,128)(2,1)S(1)} %bitcast.1060, bf16[128,6400]{1,0:T(8,128)(2,1)} %fusion.231), kind=kOutput, calls=%fused_computation.282 | convolution fusion | flops 2538758144 | bytes 41660416 | tf_op jit(solution)/shard_map/dot_general | solution.py:111
  921.4 10.7 fusion.229
  968.0 40.4 %add_add_fusion = f32[1536,6448]{1,0:T(8,128)} fusion(f32[1536,6448]{1,0:T(8,128)} %fusion.213, f32[1536,6448]{1,0:T(8,128)} %fusion.217, bf16[128,1536]{0,1:T(8,128)(2,1)S(1)} %bitcast.994, bf16[128,48]{1,0:T(8,128)(2,1)S(1)} %bitcast.1058, bf16[128,6400]{1,0:T(8,128)(2,1)S(1)} %fusion.232), kind=kOutput, calls=%fused_computation | convolution fusion | flops 2558566400 | bytes 120893440 | tf_op jit(solution)/shard_map/dot_general | solution.py:111
  1013.9 386.4 %reduce-scatter.3.cloned.1.call-done = f32[96,6448]{1,0:T(8,128)} async-done(((f32[1536,6448]{1,0:T(8,128)}), f32[96,6448]{1,0:T(8,128)}) %reduce-scatter.3.cloned.1.call-update) | async-done | bytes 2476048 | tf_op jit(solution)/shard_map/reduce_scatter | solution.py:232
  1411.3 10.4 fusion
  1422.3 110.3 %collective-permute-done.4 = f32[96,6448]{1,0:T(8,128)} collective-permute-done((f32[96,6448]{1,0:T(8,128)}, f32[96,6448]{1,0:T(8,128)}, u32[]{:S(2)}, u32[]{:S(2)}) %collective-permute-start.4) | collective-permute-done | bytes 2476064 | tf_op jit(solution)/shard_map/ppermute | solution.py:23
  1539.9 48.9 %collective-permute-done.5 = f32[96,6448]{1,0:T(8,128)} collective-permute-done((f32[96,6448]{1,0:T(8,128)}, f32[96,6448]{1,0:T(8,128)}, u32[]{:S(2)}, u32[]{:S(2)}) %collective-permute-start.5) | collective-permute-done | bytes 2476064 | tf_op jit(solution)/shard_map/ppermute | solution.py:23
  1599.1 44.6 %collective-permute-done.6 = f32[96,6448]{1,0:T(8,128)S(1)} collective-permute-done((f32[96,6448]{1,0:T(8,128)}, f32[96,6448]{1,0:T(8,128)S(1)}, u32[]{:S(2)}, u32[]{:S(2)}) %collective-permute-start.6) | collective-permute-done | bytes 2476064 | tf_op jit(solution)/shard_map/ppermute | solution.py:23
  1655.3 8.4 dynamic-slice_bitcast_fusion
  1665.6 29.1 %all-reduce.63.cloned.1.call-done = (f32[1,1536]{1,0:T(1,128)}, f32[1,4,3328]{2,1,0:T(4,128)}, f32[1,3328]{1,0:T(1,128)}, f32[1,48]{1,0:T(1,128)}, f32[1,48]{1,0...) async-done(((f32[1,1536]{1,0:T(1,128)}, f32[1,4,3328]{2,1,0:T(4,128)}, f32[1,3328]{1,0:T(1,128)}, f32[1,48]{1,0:T(1,128)}, f32[1,48]{1,0:T(1,128)}, ...) | async-done | bytes 85584 | tf_op jit(solution)/shard_map/psum | solution.py:244
  (960 shorter events, 707.2 us)
Async XLA Ops:
  7.2 129.5 %all-gather.9.cloned.1.call-start = ((), (), s32[]{:S(2)}) async-start(), calls=%async_computation.3 | async-start | bytes 24576000 | tf_op jit(solution)/shard_map/all_gather | solution.py:149
  8.0 194.5 %all-gather.11.cloned.1.call-start = ((), (), s32[]{:S(2)}) async-start(), calls=%async_computation.4 | async-start | bytes 11796480 | tf_op jit(solution)/shard_map/all_gather | solution.py:151
  8.7 1000.8 %reduce-scatter.5.cloned.1.call-start = ((), (), s32[]{:S(2)}) async-start(), calls=%async_computation.6 | async-start | bytes 20054016 | tf_op jit(solution)/shard_map/reduce_scatter | solution.py:235
  8.8 221.1 %copy-start.143 = (f32[1536]{0:T(1024)}, f32[1536]{0:T(1024)S(1)}, u32[]{:S(2)}) copy-start(f32[1536]{0:T(1024)S(1)} %reduce.80) | copy-start | bytes 18436
  15.5 753.2 %copy-start.79 = (bf16[1,1536,48]{1,2,0:T(8,128)(2,1)}, bf16[1,1536,48]{1,2,0:T(8,128)(2,1)S(1)}, u32[]{:S(2)}) copy-start(bf16[1,1536,48]{1,2,0:T(8,128)(2,1)S(1)} %all-gather.1) | copy-start | bytes 442372
  15.7 230.8 %copy-start.254 = (f32[48]{0:T(128)}, f32[48]{0:T(128)S(1)}, u32[]{:S(2)}) copy-start(f32[48]{0:T(128)S(1)} %bitcast_negate_fusion) | copy-start | bytes 580
  16.2 230.4 %copy-start.141 = (f32[128,48]{1,0:T(8,128)}, f32[128,48]{1,0:T(8,128)S(1)}, u32[]{:S(2)}) copy-start(f32[128,48]{1,0:T(8,128)S(1)} %get-tuple-element.253) | copy-start | bytes 73732
  19.3 268.7 %copy-start.136 = (f32[3072]{0:T(1024)}, f32[3072]{0:T(1024)S(1)}, u32[]{:S(2)}) copy-start(f32[3072]{0:T(1024)S(1)} %mul.1957) | copy-start | bytes 36868
  19.3 249.1 %copy-start.195 = (pred[64,64]{1,0:T(8,128)(4,1)}, pred[64,64]{1,0:T(8,128)(4,1)S(1)}, u32[]{:S(2)}) copy-start(pred[64,64]{1,0:T(8,128)(4,1)S(1)} %iota_compare_fusion) | copy-start | bytes 12292
  19.5 220.8 %copy-start.148 = (f32[3328]{0:T(1024)}, f32[3328]{0:T(1024)S(1)}, u32[]{:S(2)}) copy-start(f32[3328]{0:T(1024)S(1)} %get-tuple-element.111) | copy-start | bytes 39940
  19.5 220.8 %copy-start.153 = (f32[3328]{0:T(1024)}, f32[3328]{0:T(1024)S(1)}, u32[]{:S(2)}) copy-start(f32[3328]{0:T(1024)S(1)} %get-tuple-element.112) | copy-start | bytes 39940
  19.5 220.8 %copy-start.158 = (f32[3328]{0:T(1024)}, f32[3328]{0:T(1024)S(1)}, u32[]{:S(2)}) copy-start(f32[3328]{0:T(1024)S(1)} %get-tuple-element.113) | copy-start | bytes 39940
  19.5 220.8 %copy-start.163 = (f32[3328]{0:T(1024)}, f32[3328]{0:T(1024)S(1)}, u32[]{:S(2)}) copy-start(f32[3328]{0:T(1024)S(1)} %get-tuple-element.114) | copy-start | bytes 39940
  207.6 20.6 %collective-permute-start = (f32[128,1536]{1,0:T(8,128)S(1)}, f32[128,1536]{1,0:T(8,128)S(1)}, u32[]{:S(2)}, u32[]{:S(2)}) collective-permute-start(f32[128,1536]{1,0:T(8,128)S(1)} %fusion.150), channel_id=1, source_target_pairs={{0,16},{1,17},{2,18},{3,19},{4,20},{5,21},{6,22},{7,23},{8,24},{9,... | collective-permute-start | bytes 2359304 | tf_op jit(solution)/shard_map/ppermute | solution.py:32
  297.8 21.3 %collective-permute-start.1 = (f32[128,1536]{1,0:T(8,128)S(1)}, f32[128,1536]{1,0:T(8,128)S(1)}, u32[]{:S(2)}, u32[]{:S(2)}) collective-permute-start(f32[128,1536]{1,0:T(8,128)S(1)} %fusion.153), channel_id=1, source_target_pairs={{0,16},{1,17},{2,18},{3,19},{4,20},{5,21},{6,22},{7,23},{8,24},{9,... | collective-permute-start | bytes 2359304 | tf_op jit(solution)/shard_map/ppermute | solution.py:32
  589.6 20.9 %collective-permute-start.2 = (f32[128,1536]{1,0:T(8,128)}, f32[128,1536]{1,0:T(8,128)}, u32[]{:S(2)}, u32[]{:S(2)}) collective-permute-start(f32[128,1536]{1,0:T(8,128)} %fusion.374), channel_id=1, source_target_pairs={{16,0},{17,1},{18,2},{19,3},{20,4},{21,5},{22,6},{23,7},{24,8},{25... | collective-permute-start | bytes 2359304 | tf_op jit(solution)/shard_map/ppermute | solution.py:32
  772.8 19.9 %collective-permute-start.3 = (f32[128,1536]{1,0:T(8,128)}, f32[128,1536]{1,0:T(8,128)}, u32[]{:S(2)}, u32[]{:S(2)}) collective-permute-start(f32[128,1536]{1,0:T(8,128)} %get-tuple-element.146), channel_id=1, source_target_pairs={{16,0},{17,1},{18,2},{19,3},{20,4},{21,5},{22,6},{23,7},{24,8},{25... | collective-permute-start | bytes 2359304 | tf_op jit(solution)/shard_map/ppermute | solution.py:32
  814.0 586.3 %reduce-scatter.3.cloned.1.call-start = ((), (), s32[]{:S(2)}) async-start(), calls=%async_computation.5 | async-start | bytes 42614784 | tf_op jit(solution)/shard_map/reduce_scatter | solution.py:232
  1008.5 531.4 %all-gather.7.cloned.1.call-start = ((), (), s32[]{:S(2)}) async-start(), calls=%async_computation.2 | async-start | bytes 5898240 | tf_op jit(solution)/shard_map/all_gather | solution.py:242
  1009.5 392.1 %copy-start.77 = (bf16[1,128,3072]{2,1,0:T(8,128)(2,1)S(1)}, bf16[1,128,3072]{2,1,0:T(8,128)(2,1)}, u32[]{:S(2)}) copy-start(bf16[1,128,3072]{2,1,0:T(8,128)(2,1)} %get-tuple-element.123) | copy-start | bytes 2359300
  1009.6 685.1 %all-reduce.63.cloned.1.call-start = ((), (), s32[]{:S(2)}) async-start(), calls=%async_computation.7 | async-start | bytes 173056 | tf_op jit(solution)/shard_map/psum | solution.py:244
  1400.3 132.3 %collective-permute-start.4 = (f32[96,6448]{1,0:T(8,128)}, f32[96,6448]{1,0:T(8,128)}, u32[]{:S(2)}, u32[]{:S(2)}) collective-permute-start(f32[96,6448]{1,0:T(8,128)} %reduce-scatter.3.cloned.1.call-done), channel_id=1, source_target_pairs={{0,12},{4,0},{8,4},{12,8},{1,13},{5,1},{9,5},{13,9},{2,14},{6,2},{... | collective-permute-start | bytes 7428104 | tf_op jit(solution)/shard_map/ppermute | solution.py:23
  1532.6 56.2 %collective-permute-start.5 = (f32[96,6448]{1,0:T(8,128)}, f32[96,6448]{1,0:T(8,128)}, u32[]{:S(2)}, u32[]{:S(2)}) collective-permute-start(f32[96,6448]{1,0:T(8,128)} %collective-permute-done.4), channel_id=1, source_target_pairs={{0,12},{4,0},{8,4},{12,8},{1,13},{5,1},{9,5},{13,9},{2,14},{6,2},{... | collective-permute-start | bytes 7428104 | tf_op jit(solution)/shard_map/ppermute | solution.py:23
  1588.8 55.0 %collective-permute-start.6 = (f32[96,6448]{1,0:T(8,128)}, f32[96,6448]{1,0:T(8,128)S(1)}, u32[]{:S(2)}, u32[]{:S(2)}) collective-permute-start(f32[96,6448]{1,0:T(8,128)} %collective-permute-done.5), channel_id=1, source_target_pairs={{0,12},{4,0},{8,4},{12,8},{1,13},{5,1},{9,5},{13,9},{2,14},{6,2},{... | collective-permute-start | bytes 7428104 | tf_op jit(solution)/shard_map/ppermute | solution.py:23
  (286 other events, 4563.4 us)
Sparse Core Ops, SparseCore 0:
  9.6 127.0 all-gather.8
  138.2 64.2 all-gather.10
  814.2 195.3 reduce-scatter.4
  1013.7 386.5 reduce-scatter.2
  1401.7 130.1 all-gather.6
  1537.3 157.3 all-reduce.62
